TPU v7x, 512 devices: a whole 4x4x16 slice. The times are simulated.
512 devices in a mesh: segment: 2 (over core), lat: 64 (over x, z_lo, y), tok: 4 (over z_hi).
Axes of the slice: x: 4, y: 4, z: 16 (z_hi: 4, z_lo: 4; z = z_hi * 4 + z_lo), core: 2. Of those that a mesh axis runs over, the one named last changes fastest.
Arguments:
- resid_mid: bfloat16 [512, 4608], P('lat', ('segment', 'tok'))
- mlp_out: bfloat16 [512, 4608], P('lat', ('segment', 'tok'))
- post_gain: float32 [4608], P(('segment', 'tok')), may hold values from 0.5 to 1.5
- enc_weight: bfloat16 [4608, 65536], P(('segment', 'tok'), 'lat'), may hold values from -0.09375 to 0.09375
- enc_bias: float32 [65536], P('lat'), may hold values from -3 to 3
- dec_weight: bfloat16 [65536, 4608], P('lat', ('segment', 'tok')), may hold values from -0.046875 to 0.046875
- dec_bias: float32 [4608], P(('segment', 'tok')), may hold values from -3 to 3
- panel_lists: int32 [4, 128], replicated, may hold values from 0 to 511, as said below
Outputs:
- sq_error: float32 [], replicated
- enc_grad: bfloat16 [4608, 65536], P(('segment', 'tok'), 'lat')
- dec_grad: bfloat16 [65536, 4608], P('lat', ('segment', 'tok'))
Inputs may be any that keep to these rules, and one draw needn't show every extreme that they name: `panel_lists`: each row lists 128 different panels.
All inputs are finite; a program needn't handle non-finite values.
Results may differ from a plain program's by a relative error of at most 0.014.
Values may be sent and summed in bfloat16 or wider, within the bound.
A program may use at most 64 MiB of HBM per device.

v0:
```python
import jax
import jax.numpy as jnp
from jax import lax
from jax.sharding import PartitionSpec as P

D = 4608
PANEL = 128
BLOCK = 128


def gelu_pair(preact):
    activation, pullback = jax.vjp(jax.nn.gelu, preact)
    return (activation, pullback(jnp.ones_like(preact))[0])


def on_device(
    resid_mid, mlp_out, post_gain, enc_weight, enc_bias, dec_weight, dec_bias, panel_lists
):
    model_rows = mlp_out.astype(jnp.float32)
    squares_part = jnp.sum(model_rows * model_rows, axis=1)
    squares_total = lax.psum(squares_part, ("segment", "tok"))
    scale_rows = lax.rsqrt(squares_total / D + 1e-06)
    normed = model_rows * scale_rows[:, None] * post_gain[None, :]
    own_rows = (resid_mid.astype(jnp.float32) + normed).astype(jnp.bfloat16)
    features = lax.all_gather(own_rows, "lat", axis=0, tiled=True)
    token_count = features.shape[0]
    centered = (features.astype(jnp.float32) - dec_bias[None, :]).astype(jnp.bfloat16)
    encode_part = jnp.dot(centered, enc_weight, preferred_element_type=jnp.float32)
    preact = (
        lax.psum(encode_part.astype(jnp.bfloat16), ("segment", "tok")).astype(jnp.float32)
        + enc_bias[None, :]
    )
    panel_count = enc_weight.shape[1] // PANEL
    block_count = token_count // BLOCK
    panel_ids = lax.axis_index("lat") * panel_count + jnp.arange(panel_count, dtype=jnp.int32)
    active_flags = jnp.any(panel_lists[:, :, None] == panel_ids[None, None, :], axis=1).astype(
        jnp.float32
    )
    tile_mask = jnp.broadcast_to(
        active_flags[:, None, :, None], (block_count, BLOCK, panel_count, PANEL)
    ).reshape(token_count, enc_weight.shape[1])
    activation, derivative = gelu_pair(preact)
    latents = (activation * tile_mask).astype(jnp.bfloat16)
    decode_part = jnp.dot(latents, dec_weight, preferred_element_type=jnp.float32)
    rebuilt = lax.psum(decode_part, "lat") + dec_bias[None, :]
    error_full = rebuilt - features.astype(jnp.float32)
    error_sum = lax.psum(jnp.sum(error_full * error_full), ("segment", "tok"))
    error_bf = error_full.astype(jnp.bfloat16)
    sq_error = error_sum / (token_count * D)
    dec_grad = jnp.einsum(
        "tl,td->ld", latents, error_bf, preferred_element_type=jnp.float32
    ).astype(jnp.bfloat16)
    latent_part = jnp.einsum("td,ld->tl", error_bf, dec_weight, preferred_element_type=jnp.float32)
    latent_grad = lax.psum(latent_part.astype(jnp.bfloat16), ("segment", "tok")).astype(jnp.float32)
    pre_grad = (latent_grad * derivative * tile_mask).astype(jnp.bfloat16)
    enc_grad = jnp.einsum(
        "td,tl->dl", centered, pre_grad, preferred_element_type=jnp.float32
    ).astype(jnp.bfloat16)
    return (sq_error, enc_grad, dec_grad)


def solution(mesh):
    placed = (
        P("lat", ("segment", "tok")),
        P("lat", ("segment", "tok")),
        P(("segment", "tok")),
        P(("segment", "tok"), "lat"),
        P("lat"),
        P("lat", ("segment", "tok")),
        P(("segment", "tok")),
        P(),
    )
    return jax.shard_map(
        on_device,
        mesh=mesh,
        in_specs=placed,
        out_specs=(P(), P(("segment", "tok"), "lat"), P("lat", ("segment", "tok"))),
        check_vma=False,
    )
```

profile of v0, /device:TPU:1, one launch (start us, length us, event | category | flops | bytes accessed | tf_op | source)
XLA Modules:
  0.0 1228.6 jit_solution(12697475132606442277)
XLA Ops:
  7.2 0.0 copy-start
  7.2 0.0 all-reduce.4.cloned.1.call-start
  7.2 0.9 fusion.17
  8.1 31.2 %psum.35 = f32[8]{0:T(128)S(1)} all-reduce(f32[8]{0:T(128)S(1)} %fusion.17), channel_id=1, replica_groups=mesh['segment'=2,'lat'=64,'tok'=4] {'segment','tok'}, use_global_device_ids=true, to_apply=%region_1.0 | all-reduce | flops 8 | bytes 64 | tf_op jit(solution)/shard_map/psum | solution.py:21
  39.3 0.8 fusion.20
  40.1 160.5 %all_gather.3 = bf16[512,576]{1,0:T(8,128)(2,1)S(1)} all-gather(bf16[8,576]{1,0:T(8,128)(2,1)S(1)} %fusion.20), channel_id=1, replica_groups=mesh['segment'=2,'lat'=64,'tok'=4] {'lat'}, dimensions={0}, use_global_device_ids=true | all-gather | bytes 599040 | tf_op jit(solution)/shard_map/all_gather | solution.py:25
  200.6 0.2 copy.16
  200.9 0.0 copy-start.1
  200.9 0.0 copy-start.7
  200.9 3.6 convolution_convert_fusion.3
  204.5 0.0 copy-done.1
  204.5 0.0 copy-start.5
  204.5 0.0 all-reduce.4.cloned.1.call-update
  204.5 0.0 all-reduce.6.cloned.1.call-start
  204.6 0.0 copy-done.7
  204.6 0.2 compare_reduce_fusion
  204.8 163.0 %all-reduce.4.cloned.1.call-done = bf16[512,1024]{1,0:T(8,128)(2,1)} async-done(((bf16[512,1024]{1,0:T(8,128)(2,1)}), bf16[512,1024]{1,0:T(8,128)(2,1)}) %all-reduce.4.cloned.1.call-update) | async-done | bytes 1048592 | tf_op jit(solution)/shard_map/psum | solution.py:30
  367.8 0.0 copy-start.2
  367.8 0.2 broadcast_in_dim.2
  368.0 0.0 copy-done.5
  368.0 1.0 copy-done.2
  369.0 1.0 fusion.9
  370.0 0.0 copy-start.3
  370.0 1.0 copy-done.3
  370.9 0.0 copy-done
  370.9 0.0 copy-start.6
  370.9 1.8 fusion.27
  372.8 0.0 all-reduce.6.cloned.1.call-update
  372.8 0.0 all-reduce.8.cloned.1.call-start
  372.9 660.8 %all-reduce.6.cloned.1.call-done = f32[512,576]{0,1:T(8,128)} async-done(((f32[512,576]{0,1:T(8,128)}), f32[512,576]{0,1:T(8,128)}) %all-reduce.6.cloned.1.call-update) | async-done | bytes 1179664 | tf_op jit(solution)/shard_map/psum | solution.py:45
  1033.7 0.0 copy-done.6
  1033.7 2.5 fusion.14
  1036.2 0.0 copy-start.4
  1036.2 0.8 copy-done.4
  1037.0 2.0 convolution_convert_fusion.2
  1039.0 0.0 all-reduce.8.cloned.1.call-update
  1039.0 63.6 %psum.38 = f32[]{:T(128)} all-reduce(f32[]{:T(128)} %get-tuple-element.4), channel_id=1, replica_groups=mesh['segment'=2,'lat'=64,'tok'=4] {'segment','tok'}, use_global_device_ids=true, to_apply=%region_6.0 | all-reduce | flops 1 | bytes 8 | tf_op jit(solution)/shard_map/psum | solution.py:47
  1103.3 3.2 convolution_convert_fusion
  1106.5 109.3 %all-reduce.8.cloned.1.call-done = bf16[512,1024]{1,0:T(8,128)(2,1)} async-done(((bf16[512,1024]{1,0:T(8,128)(2,1)}), bf16[512,1024]{1,0:T(8,128)(2,1)}) %all-reduce.8.cloned.1.call-update) | async-done | bytes 1048592 | tf_op jit(solution)/shard_map/psum | solution.py:54
  1215.8 5.1 convolution_convert_fusion.1
  (3 shorter events, 0.0 us)
Async XLA Ops:
  7.2 363.8 %copy-start = (bf16[1024,576]{0,1:T(8,128)(2,1)S(1)}, bf16[1024,576]{0,1:T(8,128)(2,1)}, u32[]{:S(2)}) copy-start(bf16[1024,576]{0,1:T(8,128)(2,1)} %param.13) | copy-start | bytes 3538948
  7.2 360.6 %all-reduce.4.cloned.1.call-start = ((), (), s32[]{:S(2)}) async-start(), calls=%async_computation | async-start | bytes 2097152 | tf_op jit(solution)/shard_map/psum | solution.py:30
  200.9 3.6 copy-start.1
  200.9 3.7 copy-start.7
  204.5 163.5 %copy-start.5 = (f32[1024]{0:T(1024)S(1)}, f32[1024]{0:T(1024)}, u32[]{:S(2)}) copy-start(f32[1024]{0:T(1024)} %param.12) | copy-start | bytes 12292
  204.5 829.2 %all-reduce.6.cloned.1.call-start = ((), (), s32[]{:S(2)}) async-start(), calls=%async_computation.1 | async-start | bytes 2359296 | tf_op jit(solution)/shard_map/psum | solution.py:45
  367.8 1.2 copy-start.2
  370.0 1.0 copy-start.3
  370.9 662.7 %copy-start.6 = (f32[576]{0:T(1024)S(1)}, f32[576]{0:T(1024)}, u32[]{:S(2)}) copy-start(f32[576]{0:T(1024)} %param.14) | copy-start | bytes 6916
  372.8 843.0 %all-reduce.8.cloned.1.call-start = ((), (), s32[]{:S(2)}) async-start(), calls=%async_computation.2 | async-start | bytes 2097152 | tf_op jit(solution)/shard_map/psum | solution.py:54
  1036.2 0.8 copy-start.4
Sparse Core Ops, SparseCore 0:
  204.6 163.1 all-reduce.3
  372.9 660.7 all-reduce.5
  1039.1 176.6 all-reduce.7
where the time goes:
time: 1230 us
  waiting for transfers between devices  933 us (76%)
  blocking collectives  255 us (21%)
  matrix products  15.7 us (1%)
  between operations  15.6 us (1%)
    psum x1, waiting for transfers between devices, on_device(): rebuilt = lax.psum(decode_part, 'lat') + dec_bias[None, :]  661 us
    psum x1, waiting for transfers between devices, on_device(): lax.psum(encode_part.astype(jnp.bfloat16), ('segment', 'tok'))  163 us
    all_gather x1, blocking collectives, on_device(): features = lax.all_gather(own_rows, 'lat', axis=0, tiled=True)  161 us
    psum x1, waiting for transfers between devices, on_device(): lax.psum(latent_part.astype(jnp.bfloat16), ('segment', 'tok'))  109 us
    psum x1, blocking collectives, on_device(): error_sum = lax.psum(jnp.sum(error_full * error_full), ('segment', 'tok'))  63.6 us
    psum x1, blocking collectives, on_device(): squares_total = lax.psum(squares_part, ('segment', 'tok'))  31.2 us
  transfers between devices with their start and end apart: 3, of which 3 were waited for; matrix products, arithmetic and copies ran while one was open for 0% of the time, Pallas kernels for 0%

commit v1 on v0

v1 whole, which is shorter than its diff:
```python
import functools

import jax
import jax.numpy as jnp
from jax import lax
from jax.experimental import pallas as pl
from jax.experimental.pallas import tpu as pltpu
from jax.sharding import PartitionSpec as P

MESH = pl.DeviceIdType.MESH
D = 4608
TOKENS = 512
WIDTH = 576
LOCAL = 1024
PANELS = 8
BLOCKS = 4
BLOCK = 128
OWN = 16
STEP = 256
F32 = jnp.float32
BF16 = jnp.bfloat16
COPIES = 128


def gelu_pair(x):
    k = 0.7978845608028654
    x2 = x * x
    t = jnp.tanh(k * (x + 0.044715 * (x2 * x)))
    half = 0.5 * (1.0 + t)
    slope = half + (0.5 * x * (1.0 - t * t)) * (k * (1.0 + 0.134145 * x2))
    return x * half, slope


def nt(a, b):
    return lax.dot_general(a, b, (((1,), (1,)), ((), ())), preferred_element_type=F32)


def tn(a, b):
    return lax.dot_general(a, b, (((0,), (0,)), ((), ())), preferred_element_type=F32)


def kernel(
    slots,
    table,
    resid,
    mlp,
    gain,
    enc_bias,
    dec_bias,
    enc_w_hbm,
    dec_w_hbm,
    sq_out,
    enc_out,
    dec_out,
    enc_w,
    dec_w,
    sq_buf,
    own_rows,
    gather_y,
    feats,
    centered,
    part,
    pair_send,
    pair_recv,
    ring_send,
    ring_recv,
    slope,
    gathered,
    dense,
    decoded,
    block_own,
    xs_send,
    xs_recv,
    zs_send,
    zs_recv,
    ys_send,
    ys_recv,
    sum_buf,
    enc_v,
    dec_v,
    send_sem,
    recv_sem,
    local_sem,
):
    seg = lax.axis_index("segment")
    lat = lax.axis_index("lat")
    tok = lax.axis_index("tok")
    x = lax.div(lat, 16)
    zl = lax.rem(lax.div(lat, 4), 4)
    y = lax.rem(lat, 4)

    def turn(v, k):
        return lax.rem(v + k, 4)

    def xdev(k):
        return (seg, turn(x, k) * 16 + zl * 4 + y, tok)

    def zdev(k):
        return (seg, x * 16 + turn(zl, k) * 4 + y, tok)

    def ydev(k):
        return (seg, x * 16 + zl * 4 + turn(y, k), tok)

    def tdev(k):
        return (seg, lat, turn(tok, k))

    sibling = (1 - seg, lat, tok)
    group = [sibling] + [(s, lat, turn(tok, k)) for k in (1, 2, 3) for s in (seg, 1 - seg)]

    counter = [0]
    started = []

    def send(src, dst, device):
        i = counter[0]
        counter[0] += 1
        copy = pltpu.make_async_remote_copy(
            src_ref=src,
            dst_ref=dst,
            send_sem=send_sem.at[i],
            recv_sem=recv_sem.at[i],
            device_id=device,
            device_id_type=MESH,
        )
        copy.start()
        started.append(copy)
        return copy

    load_enc = pltpu.make_async_copy(enc_w_hbm, enc_w, local_sem.at[0])
    load_dec = pltpu.make_async_copy(dec_w_hbm, dec_w, local_sem.at[1])
    load_enc.start()
    load_dec.start()

    barrier = pltpu.get_barrier_semaphore()
    peers = group + [dev(k) for dev in (xdev, zdev, ydev) for k in (1, 2, 3)]
    for peer in peers:
        pl.semaphore_signal(barrier, inc=1, device_id=peer, device_id_type=MESH)

    rows = mlp[...].astype(F32)
    me = seg * 4 + tok
    sq_buf[0, me] = jnp.broadcast_to(jnp.sum(rows * rows, axis=1, keepdims=True), (8, 128))
    pl.semaphore_wait(barrier, len(peers))

    def group_sum(buf):
        copies = [send(buf.at[me], buf.at[me], peer) for peer in group]
        for copy in copies:
            copy.wait_recv()
        total = buf[0]
        for i in range(1, 8):
            total = total + buf[i]
        return total

    squares = group_sum(sq_buf.at[0])[:, :1]
    scale = lax.rsqrt(squares / D + 1e-06)
    own = (resid[...].astype(F32) + rows * scale * gain[...]).astype(BF16)
    own_rows[...] = own

    def ring_gather(half, v, dev):
        up = [send(half(v, 0), half(v, 0), dev(1))]
        down = [send(half(v, 1), half(v, 1), dev(3))]
        up.append(send(half(v, 1), half(v, 1), dev(1)))
        down.append(send(half(v, 0), half(v, 0), dev(3)))
        before, after = turn(v, 3), turn(v, 1)
        up[0].wait_recv()
        up.append(send(half(before, 0), half(before, 0), dev(1)))
        down[0].wait_recv()
        down.append(send(half(after, 1), half(after, 1), dev(3)))
        return up, down

    def finish(up, down):
        for copy in up[1:] + down[1:]:
            copy.wait_recv()

    def gather_all(chunk, stage, out):
        stage[y] = chunk
        copies = [send(stage.at[y], stage.at[y], ydev(k)) for k in (1, 2, 3)]
        for copy in copies:
            copy.wait_recv()
        base = pl.multiple_of((x * 4 + zl) * 32, 32)
        out[pl.ds(base, 32), :] = stage[...].reshape(32, WIDTH)
        piece = out.at[pl.ds(base, 32)]
        copies = [send(piece, piece, zdev(k)) for k in (1, 2, 3)]
        for copy in copies:
            copy.wait_recv()

        def half(v, h):
            return out.at[pl.ds(pl.multiple_of(v * BLOCK + h * 64, 64), 64)]

        finish(*ring_gather(half, x, xdev))

    gather_all(own, gather_y.at[0], feats.at[0])
    centered[...] = (feats[0].astype(F32) - dec_bias[...]).astype(BF16)

    def expand(a, weight):
        def body(n, carry):
            columns = pl.ds(pl.multiple_of(n * STEP, STEP), STEP)
            out = jnp.dot(a[...], weight[:, columns], preferred_element_type=F32)
            for i in range(STEP // BLOCK):
                piece = out[:, i * BLOCK : (i + 1) * BLOCK]
                part[n * (STEP // BLOCK) + i] = piece.reshape(TOKENS // OWN, OWN, BLOCK)
            return carry

        lax.fori_loop(0, LOCAL // STEP, body, 0)

    def reduce_slots(use, finish_tile, between=None):
        low = slots // 2
        psend, precv = pair_send.at[use], pair_recv.at[use]
        rsend, rrecv = ring_send.at[use], ring_recv.at[use]

        def loop(body, start=0, stop=slots):
            def step(c, carry):
                body(c, table[1, c], table[0, c] * 8)
                return carry

            lax.fori_loop(start, stop, step, 0)

        pair = {}
        for k in (2, 1, 3, 0):
            t = turn(tok, k)

            def to_pair(c, panel, row):
                psend[t, c] = part[panel, row + (1 - seg) * 4 + t].astype(BF16)

            loop(to_pair)
            pair[k] = send(psend.at[t], precv.at[t], sibling)

        def mine(k, c, panel, row):
            t = turn(tok, k)
            return part[panel, row + seg * 4 + t] + precv[t, c].astype(F32)

        pair[2].wait_recv()

        def far(c, panel, row):
            rsend[0, c] = mine(2, c, panel, row).astype(BF16)

        loop(far)
        first_up = send(rsend.at[0, pl.ds(0, low)], rrecv.at[0, pl.ds(0, low)], tdev(1))
        first_down = send(rsend.at[0, pl.ds(low, low)], rrecv.at[0, pl.ds(low, low)], tdev(3))
        pair[1].wait_recv()

        def near_up(c, panel, row):
            rsend[1, c] = mine(1, c, panel, row).astype(BF16)

        loop(near_up, low, slots)
        second_up = send(rsend.at[1, pl.ds(low, low)], rrecv.at[1, pl.ds(low, low)], tdev(1))
        pair[3].wait_recv()

        def near_down(c, panel, row):
            rsend[2, c] = mine(3, c, panel, row).astype(BF16)

        loop(near_down, 0, low)
        second_down = send(rsend.at[2, pl.ds(0, low)], rrecv.at[2, pl.ds(0, low)], tdev(3))

        first_up.wait_recv()

        def merged_up(c, panel, row):
            rsend[1, c] = (mine(1, c, panel, row) + rrecv[0, c].astype(F32)).astype(BF16)

        loop(merged_up, 0, low)
        third_up = send(rsend.at[1, pl.ds(0, low)], rrecv.at[1, pl.ds(0, low)], tdev(1))
        first_down.wait_recv()

        def merged_down(c, panel, row):
            rsend[2, c] = (mine(3, c, panel, row) + rrecv[0, c].astype(F32)).astype(BF16)

        loop(merged_down, low, slots)
        third_down = send(rsend.at[2, pl.ds(low, low)], rrecv.at[2, pl.ds(low, low)], tdev(3))
        pair[0].wait_recv()
        if between is not None:
            between()
        for copy in (second_up, second_down, third_up, third_down):
            copy.wait_recv()
        all_tiles = gathered.at[use]

        def last(c, panel, row):
            total = mine(0, c, panel, row) + rrecv[1, c].astype(F32) + rrecv[2, c].astype(F32)
            all_tiles[me, c] = finish_tile(c, panel, total).astype(BF16)

        loop(last)

        def half(v, h):
            return all_tiles.at[seg * 4 + v, pl.ds(h * low, low)]

        def whole(v):
            return all_tiles.at[seg * 4 + v]

        up, down = ring_gather(half, tok, tdev)
        crossing = [send(whole(tok), whole(tok), sibling)]
        up[1].wait_recv()
        before = turn(tok, 3)
        crossing.append(send(whole(before), whole(before), sibling))
        down[1].wait_recv()
        after = turn(tok, 1)
        crossing.append(send(whole(after), whole(after), sibling))
        up[2].wait_recv()
        down[2].wait_recv()
        far_side = turn(tok, 2)
        crossing.append(send(whole(far_side), whole(far_side), sibling))
        for copy in crossing:
            copy.wait_recv()

        def spread(b, carry):
            for p in range(PANELS):
                slot = table[2, b * PANELS + p]
                active = table[3, b * PANELS + p] > 0
                for j in range(8):
                    tile = all_tiles[j, slot]
                    at = pl.multiple_of(b * BLOCK + j * OWN, OWN)
                    dense[use, pl.ds(at, OWN), p * BLOCK : (p + 1) * BLOCK] = jnp.where(
                        active, tile, jnp.zeros_like(tile)
                    )
            return carry

        lax.fori_loop(0, BLOCKS, spread, 0)

    load_enc.wait()
    expand(centered, enc_w)

    def latents_of(c, panel, total):
        activation, derivative = gelu_pair(total + enc_bias[pl.ds(panel, 1), :])
        slope[c] = derivative
        return activation

    reduce_slots(0, latents_of)

    load_dec.wait()
    latents = dense.at[0]

    def decode_block(k, carry):
        b = pl.multiple_of(turn(x, k) * BLOCK, BLOCK)
        decoded[k] = nt(latents[pl.ds(b, BLOCK), :], dec_w[...])
        return carry

    lax.fori_loop(0, BLOCKS, decode_block, 0)

    def decode(k):
        return decoded[k]

    far = decode(2)
    xs_send[0] = far.astype(BF16)
    first_up = send(xs_send.at[0, pl.ds(0, 64)], xs_recv.at[0, pl.ds(0, 64)], xdev(1))
    first_down = send(xs_send.at[0, pl.ds(64, 64)], xs_recv.at[0, pl.ds(64, 64)], xdev(3))
    near = decode(1)
    xs_send[1, 64:, :] = near[64:, :].astype(BF16)
    second_up = send(xs_send.at[1, pl.ds(64, 64)], xs_recv.at[1, pl.ds(64, 64)], xdev(1))
    block_own[0:64, :] = near[:64, :]
    near = decode(3)
    xs_send[2, :64, :] = near[:64, :].astype(BF16)
    second_down = send(xs_send.at[2, pl.ds(0, 64)], xs_recv.at[2, pl.ds(0, 64)], xdev(3))
    block_own[64:128, :] = near[64:, :]
    first_up.wait_recv()
    xs_send[1, :64, :] = (block_own[0:64, :] + xs_recv[0, :64, :].astype(F32)).astype(BF16)
    third_up = send(xs_send.at[1, pl.ds(0, 64)], xs_recv.at[1, pl.ds(0, 64)], xdev(1))
    first_down.wait_recv()
    xs_send[2, 64:, :] = (block_own[64:128, :] + xs_recv[0, 64:, :].astype(F32)).astype(BF16)
    third_down = send(xs_send.at[2, pl.ds(64, 64)], xs_recv.at[2, pl.ds(64, 64)], xdev(3))
    block_own[...] = decode(0)
    for copy in (second_up, second_down, third_up, third_down):
        copy.wait_recv()
    block_own[...] = block_own[...] + xs_recv[1].astype(F32) + xs_recv[2].astype(F32)

    copies = []
    for k in (1, 2, 3):
        at = pl.multiple_of(turn(zl, k) * 32, 32)
        zs_send[k - 1] = block_own[pl.ds(at, 32), :].astype(BF16)
        copies.append(send(zs_send.at[k - 1], zs_recv.at[k - 1], zdev(k)))
    quarter = block_own[pl.ds(pl.multiple_of(zl * 32, 32), 32), :]
    for k in (1, 2, 3):
        copies[k - 1].wait_recv()
        quarter = quarter + zs_recv[k - 1].astype(F32)
    block_own[0:32, :] = quarter
    copies = []
    for k in (1, 2, 3):
        at = pl.multiple_of(turn(y, k) * 8, 8)
        ys_send[k - 1] = block_own[pl.ds(at, 8), :].astype(BF16)
        copies.append(send(ys_send.at[k - 1], ys_recv.at[k - 1], ydev(k)))
    rebuilt = block_own[pl.ds(pl.multiple_of(y * 8, 8), 8), :]
    for k in (1, 2, 3):
        copies[k - 1].wait_recv()
        rebuilt = rebuilt + ys_recv[k - 1].astype(F32)

    error = rebuilt + dec_bias[...] - own_rows[...].astype(F32)
    gather_all(error.astype(BF16), gather_y.at[1], feats.at[1])
    errors = feats.at[1]

    squared = jnp.sum(error * error, axis=1, keepdims=True)
    squared = jnp.sum(squared, axis=0, keepdims=True)
    loss = jnp.broadcast_to(squared, (8, 128))

    def loss_step(i, v, dev, value):
        sum_buf[i, v] = value
        return [send(sum_buf.at[i, v], sum_buf.at[i, v], dev(k)) for k in (1, 2, 3)]

    def loss_sum(i, copies):
        for copy in copies:
            copy.wait_recv()
        return (sum_buf[i, 0] + sum_buf[i, 1]) + (sum_buf[i, 2] + sum_buf[i, 3])

    expand(errors, dec_w)
    for i, v, dev in ((0, y, ydev), (1, zl, zdev), (2, x, xdev)):
        loss = loss_sum(i, loss_step(i, v, dev, loss))
    sq_buf[1, me] = loss
    sq_out[...] = group_sum(sq_buf.at[1]) / (TOKENS * D)

    store_dec = pltpu.make_async_copy(dec_v, dec_out, local_sem.at[2])
    store_enc = pltpu.make_async_copy(enc_v, enc_out, local_sem.at[3])

    def outer(a, use, result):
        def body(n, carry):
            columns = pl.ds(pl.multiple_of(n * STEP, STEP), STEP)
            result[:, columns] = tn(a[...], dense[use, :, columns]).astype(BF16)
            return carry

        lax.fori_loop(0, LOCAL // STEP, body, 0)

    def decoder_gradient():
        outer(errors, 0, dec_v)
        store_dec.start()

    reduce_slots(1, lambda c, panel, total: total * slope[c], decoder_gradient)
    outer(centered, 1, enc_v)
    store_enc.start()
    store_dec.wait()
    store_enc.wait()
    for copy in started:
        copy.wait_send()


def step(slots, table, resid_mid, mlp_out, post_gain, enc_weight, enc_bias, dec_weight, dec_bias):
    vmem = pl.BlockSpec(memory_space=pltpu.VMEM)
    anywhere = pl.BlockSpec(memory_space=pl.ANY)
    low = pltpu.VMEM
    return pl.pallas_call(
        functools.partial(kernel, slots),
        name="sae_step",
        out_shape=(
            jax.ShapeDtypeStruct((8, 128), F32),
            jax.ShapeDtypeStruct((WIDTH, LOCAL), BF16),
            jax.ShapeDtypeStruct((WIDTH, LOCAL), BF16),
        ),
        in_specs=[pl.BlockSpec(memory_space=pltpu.SMEM)] + [vmem] * 5 + [anywhere] * 2,
        out_specs=(vmem, anywhere, anywhere),
        scratch_shapes=[
            low((WIDTH, LOCAL), BF16),
            low((WIDTH, LOCAL), BF16),
            low((2, 8, 8, 128), F32),
            low((8, WIDTH), BF16),
            low((2, 4, 8, WIDTH), BF16),
            low((2, TOKENS, WIDTH), BF16),
            low((TOKENS, WIDTH), BF16),
            low((PANELS, TOKENS // OWN, OWN, BLOCK), F32),
            low((2, 4, slots, OWN, BLOCK), BF16),
            low((2, 4, slots, OWN, BLOCK), BF16),
            low((2, 3, slots, OWN, BLOCK), BF16),
            low((2, 3, slots, OWN, BLOCK), BF16),
            low((slots, OWN, BLOCK), F32),
            low((2, 8, slots, OWN, BLOCK), BF16),
            low((2, TOKENS, LOCAL), BF16),
            low((BLOCKS, BLOCK, WIDTH), F32),
            low((BLOCK, WIDTH), F32),
            low((3, BLOCK, WIDTH), BF16),
            low((3, BLOCK, WIDTH), BF16),
            low((3, 32, WIDTH), BF16),
            low((3, 32, WIDTH), BF16),
            low((3, 8, WIDTH), BF16),
            low((3, 8, WIDTH), BF16),
            low((3, 4, 8, 128), F32),
            low((WIDTH, LOCAL), BF16),
            low((WIDTH, LOCAL), BF16),
            pltpu.SemaphoreType.DMA((COPIES,)),
            pltpu.SemaphoreType.DMA((COPIES,)),
            pltpu.SemaphoreType.DMA((4,)),
        ],
        compiler_params=pltpu.CompilerParams(
            collective_id=0, has_side_effects=True, vmem_limit_bytes=48 * 1024 * 1024
        ),
    )(
        table,
        resid_mid,
        mlp_out,
        post_gain.reshape(1, WIDTH),
        enc_bias.reshape(PANELS, BLOCK),
        dec_bias.reshape(1, WIDTH),
        enc_weight,
        dec_weight.T,
    )


def tables(panel_lists):
    ids = lax.axis_index("lat") * PANELS + jnp.arange(PANELS, dtype=jnp.int32)
    active = jnp.any(panel_lists[:, :, None] == ids[None, None, :], axis=1).reshape(-1)
    active = active.astype(jnp.int32)
    tiles = jnp.arange(BLOCKS * PANELS, dtype=jnp.int32)
    rank = jnp.sum(jnp.where(tiles[None, :] < tiles[:, None], active[None, :], 0), axis=1)
    here = (rank[None, :] == tiles[:, None]) & (active[None, :] > 0)
    tile = jnp.sum(jnp.where(here, tiles[None, :], 0), axis=1)
    slot = jnp.where(active > 0, rank, 0)
    return jnp.stack([tile // PANELS, tile % PANELS, slot, active]).astype(jnp.int32)


def on_device(
    resid_mid, mlp_out, post_gain, enc_weight, enc_bias, dec_weight, dec_bias, panel_lists
):
    table = tables(panel_lists)
    loss, enc_grad, dec_grad = step(
        32, table, resid_mid, mlp_out, post_gain, enc_weight, enc_bias, dec_weight, dec_bias
    )
    return loss[0, 0], enc_grad, dec_grad.T


def solution(mesh):
    placed = (
        P("lat", ("segment", "tok")),
        P("lat", ("segment", "tok")),
        P(("segment", "tok")),
        P(("segment", "tok"), "lat"),
        P("lat"),
        P("lat", ("segment", "tok")),
        P(("segment", "tok")),
        P(),
    )
    return jax.shard_map(
        on_device,
        mesh=mesh,
        in_specs=placed,
        out_specs=(P(), P(("segment", "tok"), "lat"), P("lat", ("segment", "tok"))),
        check_vma=False,
    )
```

time: 1230 us -> 207 us (0.17)
  waiting for transfers between devices: 933 us -> 0 us
  blocking collectives: 255 us -> 0 us
  Pallas kernels: 0 us -> 196 us
  matrix products: 15.7 us -> 0 us
  between operations: 15.6 us -> 0.69 us
    psum x3 -> x0, waiting for transfers between devices: 933 us -> none  [the longest x1 661 us: on_device(): rebuilt = lax.psum(decode_part, 'lat') + dec_bias[None, :]]
    pallas_call x0 -> x1, Pallas kernels: none -> 196 us  [step(): pl.pallas_call(functools.partial(kernel, slots), name='sae_step', out_sha...]
    all_gather x1 -> x0, blocking collectives: 161 us -> none  [on_device(): features = lax.all_gather(own_rows, 'lat', axis=0, tiled=True)]
    psum x2 -> x0, blocking collectives: 94.8 us -> none  [the longest x1 63.6 us: on_device(): error_sum = lax.psum(jnp.sum(error_full * error_full), ('segment', 'tok'))]
    dot_general x5 -> x0, matrix products: 15.7 us -> none  [the longest x1 5.11 us: on_device(): jnp.einsum('td,tl->dl', centered, pre_grad, preferred_element_type=jnp.fl...]
  transfers between devices with their start and end apart: 3 -> 0, of which waited for: 3 -> 0; matrix products, arithmetic and copies ran while one was open for 0% -> 0% of each run, Pallas kernels for 0% -> 0%
where the time goes in v1:
time: 207 us; the launch traced here: 206 us
  Pallas kernels  196 us (95%)
  local copies, waits for them, and re-layouts  8.71 us (4%)
    pallas_call x1, Pallas kernels, step(): pl.pallas_call(functools.partial(kernel, slots), name='sae_step', out_sha...  196 us
    unnamed x12, local copies, waits for them, and re-layouts  6.65 us

profile of v1, /device:TPU:1, one launch (start us, length us, event | category | flops | bytes accessed | tf_op | source)
XLA Modules:
  0.0 206.3 jit_solution(1876009316991602836)
XLA Ops:
  0.6 0.9 compare_reduce_fusion
  1.5 0.1 reshape.131
  1.6 0.1 reshape.130
  1.7 0.1 select_reduce_fusion.1
  1.8 0.1 select_reduce_fusion
  2.0 0.7 reshape.127.gain
  2.7 0.7 reshape.129.dec_bias
  3.4 0.0 copy-start
  3.4 1.3 copy-done
  4.7 0.0 copy-start.1
  4.7 1.3 copy-done.1
  5.9 0.0 copy-start.2
  5.9 0.7 copy-done.2
  6.6 0.0 copy-start.3
  6.6 0.7 copy-done.3
  7.3 0.0 copy-start.4
  7.3 0.7 copy-done.4
  8.0 195.7 %sae_step.1 = (f32[8,128]{1,0:T(8,128)S(1)}, bf16[576,1024]{1,0:T(8,128)(2,1)S(1)}, bf16[576,1024]{1,0:T(8,128)(2,1)S(1)}) custom-call(s32[4,32]{1,0:T(4,128)S(1)} %pad_add_fusion.table, bf16[8,576]{1,0:T(8,128)(2,1)S(1)} %copy-done.2, bf16[8,576]{1,0:T(8,128)(2,1)S(1)} %copy-done.3, f32[1,576]{1,0:T(1,128)S(1)} %reshape.127.gain, f32[8,128]{1,0:T(8,128)S(1)} %bitcast.23, ...), custom_call_target="tpu_custom_call" | custom-call | tf_op jit(solution)/shard_map/sae_step/pallas_call | solution.py:432
  203.8 0.5 slice.3
  204.3 1.0 copy.13
  205.3 1.0 copy.14
  (5 shorter events, 0.0 us)
Async XLA Ops:
  3.4 1.3 copy-start
  4.7 1.3 copy-start.1
  5.9 0.7 copy-start.2
  6.6 0.7 copy-start.3
  7.3 0.7 copy-start.4

commit v2 on v1

--- a/solution.py
+++ b/solution.py
@@ -20,6 +20,7 @@
 F32 = jnp.float32
 BF16 = jnp.bfloat16
 COPIES = 128
+CAPACITIES = (16, 20, 32)
 
 
 def gelu_pair(x):
@@ -42,16 +43,21 @@
 def kernel(
     slots,
     table,
+    resid_hbm,
+    mlp_hbm,
+    gain_hbm,
+    enc_bias_hbm,
+    dec_bias_hbm,
+    enc_w_hbm,
+    dec_w_hbm,
+    sq_out,
+    enc_out,
+    dec_out,
     resid,
     mlp,
     gain,
     enc_bias,
     dec_bias,
-    enc_w_hbm,
-    dec_w_hbm,
-    sq_out,
-    enc_out,
-    dec_out,
     enc_w,
     dec_w,
     sq_buf,
@@ -125,23 +131,40 @@
         started.append(copy)
         return copy
 
-    load_enc = pltpu.make_async_copy(enc_w_hbm, enc_w, local_sem.at[0])
-    load_dec = pltpu.make_async_copy(dec_w_hbm, dec_w, local_sem.at[1])
-    load_enc.start()
-    load_dec.start()
+    loads = [
+        pltpu.make_async_copy(src, dst, local_sem.at[i])
+        for i, (src, dst) in enumerate(
+            (
+                (mlp_hbm, mlp),
+                (resid_hbm, resid),
+                (gain_hbm, gain),
+                (enc_bias_hbm, enc_bias),
+                (dec_bias_hbm, dec_bias),
+                (enc_w_hbm, enc_w),
+                (dec_w_hbm, dec_w),
+            )
+        )
+    ]
+    for load in loads:
+        load.start()
 
     barrier = pltpu.get_barrier_semaphore()
     peers = group + [dev(k) for dev in (xdev, zdev, ydev) for k in (1, 2, 3)]
     for peer in peers:
         pl.semaphore_signal(barrier, inc=1, device_id=peer, device_id_type=MESH)
 
+    loads[0].wait()
     rows = mlp[...].astype(F32)
     me = seg * 4 + tok
     sq_buf[0, me] = jnp.broadcast_to(jnp.sum(rows * rows, axis=1, keepdims=True), (8, 128))
     pl.semaphore_wait(barrier, len(peers))
-
-    def group_sum(buf):
-        copies = [send(buf.at[me], buf.at[me], peer) for peer in group]
+    for load in loads[1:]:
+        load.wait()
+
+    def group_start(buf):
+        return [send(buf.at[me], buf.at[me], peer) for peer in group]
+
+    def group_sum(buf, copies):
         for copy in copies:
             copy.wait_recv()
         total = buf[0]
@@ -149,7 +172,7 @@
             total = total + buf[i]
         return total
 
-    squares = group_sum(sq_buf.at[0])[:, :1]
+    squares = group_sum(sq_buf.at[0], group_start(sq_buf.at[0]))[:, :1]
     scale = lax.rsqrt(squares / D + 1e-06)
     own = (resid[...].astype(F32) + rows * scale * gain[...]).astype(BF16)
     own_rows[...] = own
@@ -166,26 +189,41 @@
         down.append(send(half(after, 1), half(after, 1), dev(3)))
         return up, down
 
-    def finish(up, down):
-        for copy in up[1:] + down[1:]:
-            copy.wait_recv()
-
-    def gather_all(chunk, stage, out):
+    def gather_all(chunk, stage, out, side=None):
+        def side_start(i, v, dev, value):
+            if side is None:
+                return None
+            sum_buf[i, v] = value
+            return [send(sum_buf.at[i, v], sum_buf.at[i, v], dev(k)) for k in (1, 2, 3)]
+
+        def side_sum(i, copies):
+            if side is None:
+                return None
+            for copy in copies:
+                copy.wait_recv()
+            return (sum_buf[i, 0] + sum_buf[i, 1]) + (sum_buf[i, 2] + sum_buf[i, 3])
+
         stage[y] = chunk
         copies = [send(stage.at[y], stage.at[y], ydev(k)) for k in (1, 2, 3)]
+        beside = side_start(0, y, ydev, side)
         for copy in copies:
             copy.wait_recv()
         base = pl.multiple_of((x * 4 + zl) * 32, 32)
         out[pl.ds(base, 32), :] = stage[...].reshape(32, WIDTH)
         piece = out.at[pl.ds(base, 32)]
         copies = [send(piece, piece, zdev(k)) for k in (1, 2, 3)]
+        beside = side_start(1, zl, zdev, side_sum(0, beside))
         for copy in copies:
             copy.wait_recv()
 
         def half(v, h):
             return out.at[pl.ds(pl.multiple_of(v * BLOCK + h * 64, 64), 64)]
 
-        finish(*ring_gather(half, x, xdev))
+        up, down = ring_gather(half, x, xdev)
+        beside = side_start(2, x, xdev, side_sum(1, beside))
+        for copy in up[1:] + down[1:]:
+            copy.wait_recv()
+        return side_sum(2, beside)
 
     gather_all(own, gather_y.at[0], feats.at[0])
     centered[...] = (feats[0].astype(F32) - dec_bias[...]).astype(BF16)
@@ -312,7 +350,6 @@
 
         lax.fori_loop(0, BLOCKS, spread, 0)
 
-    load_enc.wait()
     expand(centered, enc_w)
 
     def latents_of(c, panel, total):
@@ -322,7 +359,6 @@
 
     reduce_slots(0, latents_of)
 
-    load_dec.wait()
     latents = dense.at[0]
 
     def decode_block(k, carry):
@@ -379,30 +415,17 @@
         rebuilt = rebuilt + ys_recv[k - 1].astype(F32)
 
     error = rebuilt + dec_bias[...] - own_rows[...].astype(F32)
-    gather_all(error.astype(BF16), gather_y.at[1], feats.at[1])
+    squared = jnp.sum(jnp.sum(error * error, axis=1, keepdims=True), axis=0, keepdims=True)
+    loss = gather_all(
+        error.astype(BF16), gather_y.at[1], feats.at[1], jnp.broadcast_to(squared, (8, 128))
+    )
     errors = feats.at[1]
-
-    squared = jnp.sum(error * error, axis=1, keepdims=True)
-    squared = jnp.sum(squared, axis=0, keepdims=True)
-    loss = jnp.broadcast_to(squared, (8, 128))
-
-    def loss_step(i, v, dev, value):
-        sum_buf[i, v] = value
-        return [send(sum_buf.at[i, v], sum_buf.at[i, v], dev(k)) for k in (1, 2, 3)]
-
-    def loss_sum(i, copies):
-        for copy in copies:
-            copy.wait_recv()
-        return (sum_buf[i, 0] + sum_buf[i, 1]) + (sum_buf[i, 2] + sum_buf[i, 3])
+    sq_buf[1, me] = loss
+    loss_copies = group_start(sq_buf.at[1])
 
     expand(errors, dec_w)
-    for i, v, dev in ((0, y, ydev), (1, zl, zdev), (2, x, xdev)):
-        loss = loss_sum(i, loss_step(i, v, dev, loss))
-    sq_buf[1, me] = loss
-    sq_out[...] = group_sum(sq_buf.at[1]) / (TOKENS * D)
-
-    store_dec = pltpu.make_async_copy(dec_v, dec_out, local_sem.at[2])
-    store_enc = pltpu.make_async_copy(enc_v, enc_out, local_sem.at[3])
+    store_dec = pltpu.make_async_copy(dec_v, dec_out, local_sem.at[7])
+    store_enc = pltpu.make_async_copy(enc_v, enc_out, local_sem.at[8])
 
     def outer(a, use, result):
         def body(n, carry):
@@ -415,6 +438,7 @@
     def decoder_gradient():
         outer(errors, 0, dec_v)
         store_dec.start()
+        sq_out[...] = group_sum(sq_buf.at[1], loss_copies) / (TOKENS * D)
 
     reduce_slots(1, lambda c, panel, total: total * slope[c], decoder_gradient)
     outer(centered, 1, enc_v)
@@ -425,21 +449,26 @@
         copy.wait_send()
 
 
-def step(slots, table, resid_mid, mlp_out, post_gain, enc_weight, enc_bias, dec_weight, dec_bias):
+def step(place, slots, table, resid_mid, mlp_out, post_gain, enc_weight, enc_bias, dec_weight, dec_bias):
     vmem = pl.BlockSpec(memory_space=pltpu.VMEM)
-    anywhere = pl.BlockSpec(memory_space=pl.ANY)
+    hbm = pl.BlockSpec(memory_space=pltpu.HBM)
     low = pltpu.VMEM
     return pl.pallas_call(
         functools.partial(kernel, slots),
-        name="sae_step",
+        name=f"sae_step_{slots}",
         out_shape=(
             jax.ShapeDtypeStruct((8, 128), F32),
             jax.ShapeDtypeStruct((WIDTH, LOCAL), BF16),
             jax.ShapeDtypeStruct((WIDTH, LOCAL), BF16),
         ),
-        in_specs=[pl.BlockSpec(memory_space=pltpu.SMEM)] + [vmem] * 5 + [anywhere] * 2,
-        out_specs=(vmem, anywhere, anywhere),
+        in_specs=[pl.BlockSpec(memory_space=pltpu.SMEM)] + [hbm] * 7,
+        out_specs=(vmem, hbm, hbm),
         scratch_shapes=[
+            low((8, WIDTH), BF16),
+            low((8, WIDTH), BF16),
+            low((1, WIDTH), F32),
+            low((PANELS, BLOCK), F32),
+            low((1, WIDTH), F32),
             low((WIDTH, LOCAL), BF16),
             low((WIDTH, LOCAL), BF16),
             low((2, 8, 8, 128), F32),
@@ -468,10 +497,10 @@
             low((WIDTH, LOCAL), BF16),
             pltpu.SemaphoreType.DMA((COPIES,)),
             pltpu.SemaphoreType.DMA((COPIES,)),
-            pltpu.SemaphoreType.DMA((4,)),
+            pltpu.SemaphoreType.DMA((9,)),
         ],
         compiler_params=pltpu.CompilerParams(
-            collective_id=0, has_side_effects=True, vmem_limit_bytes=48 * 1024 * 1024
+            collective_id=place, has_side_effects=True, vmem_limit_bytes=48 * 1024 * 1024
         ),
     )(
         table,
@@ -501,8 +530,20 @@
     resid_mid, mlp_out, post_gain, enc_weight, enc_bias, dec_weight, dec_bias, panel_lists
 ):
     table = tables(panel_lists)
-    loss, enc_grad, dec_grad = step(
-        32, table, resid_mid, mlp_out, post_gain, enc_weight, enc_bias, dec_weight, dec_bias
+    groups = jnp.arange(lax.axis_size("lat"), dtype=jnp.int32)
+    per_group = jnp.sum(panel_lists.reshape(1, -1) // PANELS == groups[:, None], axis=1)
+    most = jnp.max(per_group)
+    loss, enc_grad, dec_grad = lax.switch(
+        sum((most > slots).astype(jnp.int32) for slots in CAPACITIES[:-1]),
+        [functools.partial(step, i, slots) for i, slots in enumerate(CAPACITIES)],
+        table,
+        resid_mid,
+        mlp_out,
+        post_gain,
+        enc_weight,
+        enc_bias,
+        dec_weight,
+        dec_bias,
     )
     return loss[0, 0], enc_grad, dec_grad.T
 

time: 207 us -> 152 us (0.73)
  Pallas kernels: 196 us -> 141 us
  local copies, waits for them, and re-layouts: 8.71 us -> 4.08 us
    pallas_call x1, Pallas kernels: 196 us -> 141 us  [step(): pl.pallas_call(functools.partial(kernel, slots), name=f'sae_step_{slots}'...]
    unnamed x12 -> x2, local copies, waits for them, and re-layouts: 6.65 us -> 2.03 us
where the time goes in v2:
time: 152 us; the launch traced here: 150 us
  Pallas kernels  141 us (93%)
  local copies, waits for them, and re-layouts  4.08 us (3%)
  other arithmetic  2.61 us (2%)
  between operations  1.98 us (1%)
    pallas_call x1, Pallas kernels, step(): pl.pallas_call(functools.partial(kernel, slots), name=f'sae_step_{slots}'...  141 us

profile of v2, /device:TPU:1, one launch (start us, length us, event | category | flops | bytes accessed | tf_op | source)
XLA Modules:
  0.0 150.0 jit_solution(18215744346865502010)
XLA Ops:
  0.6 0.9 compare_reduce_fusion
  1.5 0.1 reshape.209
  1.6 0.1 reshape.208
  1.7 0.1 select_reduce_fusion.1
  1.8 0.1 select_reduce_fusion
  2.0 0.7 add_select_fusion
  2.7 0.1 convert_reduce_fusion
  2.8 0.6 reduce_max.9
  4.8 143.2 %conditional.1 = (bf16[576,1024]{1,0:T(8,128)(2,1)S(1)}, bf16[576,1024]{1,0:T(8,128)(2,1)S(1)}, f32[]{:T(128)}) conditional(s32[]{:T(128)} %clamp.3, (f32[576]{0:T(1024)}, f32[1024]{0:T(1024)}, f32[576]{0:T(1024)}, bf16[1024,576]{0,1:T(8,128)(2,1)}, s32[4,32]{1,0:T(4,128)S(1)}, /*index=5*/bf16[8,576]{1,0:T(8,128)(2,1)}, ...), branch_computations={%region_5.6_spmd, %region_6.7_spmd, %region_7.8_spmd} | conditional | bytes 9248 | solution.py:536
  4.8 0.7 reshape.197.gain_hbm
  5.5 0.7 reshape.199.dec_bias_hbm
  6.1 141.3 %sae_step_16.1 = (f32[8,128]{1,0:T(8,128)S(1)}, bf16[576,1024]{1,0:T(8,128)(2,1)S(1)}, bf16[576,1024]{1,0:T(8,128)(2,1)S(1)}) custom-call(s32[4,32]{1,0:T(4,128)S(1)} %get-tuple-element.58.table, bf16[8,576]{1,0:T(8,128)(2,1)} %get-tuple-element.59.resid_hbm, bf16[8,576]{1,0:T(8,128)(2,1)} %get-tuple-element.60.mlp_hbm, f32[1,576]{1,0:T(1,128)S(1)} %reshape.197.gain_hbm, ...), custom_call_target="tpu_custom_call" | custom-call | tf_op jit(solution)/shard_map/cond/branch_0_fun/sae_step_16/pallas_call | solution.py:456
  147.5 0.5 slice.7
  148.0 1.0 copy.22
  149.0 1.0 copy.23
  (5 shorter events, 0.0 us)

commit v3 on v2

--- a/solution.py
+++ b/solution.py
@@ -19,8 +19,8 @@
 STEP = 256
 F32 = jnp.float32
 BF16 = jnp.bfloat16
-COPIES = 128
-CAPACITIES = (16, 20, 32)
+COPIES = 192
+CAPACITIES = (20, 32)
 
 
 def gelu_pair(x):
@@ -77,10 +77,8 @@
     block_own,
     xs_send,
     xs_recv,
-    zs_send,
-    zs_recv,
-    ys_send,
-    ys_recv,
+    ps_send,
+    ps_recv,
     sum_buf,
     enc_v,
     dec_v,
@@ -101,11 +99,20 @@
     def xdev(k):
         return (seg, turn(x, k) * 16 + zl * 4 + y, tok)
 
+    def plane(i, j):
+        return turn(zl, i) * 4 + turn(y, j)
+
+    near = [(i, j) for i in range(4) for j in range(4) if i or j]
+    spot = zl * 4 + y
+
+    def ydev(k):
+        return pdev(0, k)
+
     def zdev(k):
-        return (seg, x * 16 + turn(zl, k) * 4 + y, tok)
-
-    def ydev(k):
-        return (seg, x * 16 + zl * 4 + turn(y, k), tok)
+        return pdev(k, 0)
+
+    def pdev(i, j):
+        return (seg, x * 16 + plane(i, j), tok)
 
     def tdev(k):
         return (seg, lat, turn(tok, k))
@@ -149,7 +156,7 @@
         load.start()
 
     barrier = pltpu.get_barrier_semaphore()
-    peers = group + [dev(k) for dev in (xdev, zdev, ydev) for k in (1, 2, 3)]
+    peers = group + [xdev(k) for k in (1, 2, 3)] + [pdev(i, j) for i, j in near]
     for peer in peers:
         pl.semaphore_signal(barrier, inc=1, device_id=peer, device_id_type=MESH)
 
@@ -158,7 +165,7 @@
     me = seg * 4 + tok
     sq_buf[0, me] = jnp.broadcast_to(jnp.sum(rows * rows, axis=1, keepdims=True), (8, 128))
     pl.semaphore_wait(barrier, len(peers))
-    for load in loads[1:]:
+    for load in loads[1:7]:
         load.wait()
 
     def group_start(buf):
@@ -177,16 +184,23 @@
     own = (resid[...].astype(F32) + rows * scale * gain[...]).astype(BF16)
     own_rows[...] = own
 
-    def ring_gather(half, v, dev):
-        up = [send(half(v, 0), half(v, 0), dev(1))]
-        down = [send(half(v, 1), half(v, 1), dev(3))]
-        up.append(send(half(v, 1), half(v, 1), dev(1)))
-        down.append(send(half(v, 0), half(v, 0), dev(3)))
+    def ring_gather(piece, cuts, v, dev):
+        a, b, c, d = cuts
+
+        def pass_on(owner, start, stop, k):
+            ref = piece(owner, start, stop)
+            return send(ref, ref, dev(k))
+
+        up = [pass_on(v, 0, a, 1), pass_on(v, a, b, 1)]
+        down = [pass_on(v, b, c, 3), pass_on(v, c, d, 3)]
+        up.append(pass_on(v, b, d, 1))
+        down.append(pass_on(v, 0, b, 3))
         before, after = turn(v, 3), turn(v, 1)
-        up[0].wait_recv()
-        up.append(send(half(before, 0), half(before, 0), dev(1)))
-        down[0].wait_recv()
-        down.append(send(half(after, 1), half(after, 1), dev(3)))
+        for i, low, high in ((0, (0, a), (b, c)), (1, (a, b), (c, d))):
+            up[i].wait_recv()
+            up.append(pass_on(before, *low, 1))
+            down[i].wait_recv()
+            down.append(pass_on(after, *high, 3))
         return up, down
 
     def gather_all(chunk, stage, out, side=None):
@@ -203,27 +217,21 @@
                 copy.wait_recv()
             return (sum_buf[i, 0] + sum_buf[i, 1]) + (sum_buf[i, 2] + sum_buf[i, 3])
 
-        stage[y] = chunk
-        copies = [send(stage.at[y], stage.at[y], ydev(k)) for k in (1, 2, 3)]
+        stage[spot] = chunk
+        copies = [send(stage.at[spot], stage.at[spot], pdev(i, j)) for i, j in near]
         beside = side_start(0, y, ydev, side)
         for copy in copies:
             copy.wait_recv()
-        base = pl.multiple_of((x * 4 + zl) * 32, 32)
-        out[pl.ds(base, 32), :] = stage[...].reshape(32, WIDTH)
-        piece = out.at[pl.ds(base, 32)]
-        copies = [send(piece, piece, zdev(k)) for k in (1, 2, 3)]
+        out[pl.ds(pl.multiple_of(x * BLOCK, BLOCK), BLOCK), :] = stage[...].reshape(BLOCK, WIDTH)
+
+        def piece(v, start, stop):
+            return out.at[pl.ds(pl.multiple_of(v * BLOCK + start, 32), stop - start)]
+
+        up, down = ring_gather(piece, (32, 64, 96, 128), x, xdev)
         beside = side_start(1, zl, zdev, side_sum(0, beside))
-        for copy in copies:
+        for copy in up[2:] + down[2:]:
             copy.wait_recv()
-
-        def half(v, h):
-            return out.at[pl.ds(pl.multiple_of(v * BLOCK + h * 64, 64), 64)]
-
-        up, down = ring_gather(half, x, xdev)
-        beside = side_start(2, x, xdev, side_sum(1, beside))
-        for copy in up[1:] + down[1:]:
-            copy.wait_recv()
-        return side_sum(2, beside)
+        return side_start(2, x, xdev, side_sum(1, beside)), side_sum
 
     gather_all(own, gather_y.at[0], feats.at[0])
     centered[...] = (feats[0].astype(F32) - dec_bias[...]).astype(BF16)
@@ -270,42 +278,51 @@
         def far(c, panel, row):
             rsend[0, c] = mine(2, c, panel, row).astype(BF16)
 
-        loop(far)
-        first_up = send(rsend.at[0, pl.ds(0, low)], rrecv.at[0, pl.ds(0, low)], tdev(1))
-        first_down = send(rsend.at[0, pl.ds(low, low)], rrecv.at[0, pl.ds(low, low)], tdev(3))
+        def ring(i, start, stop, k):
+            span = pl.ds(start, stop - start)
+            return send(rsend.at[i, span], rrecv.at[i, span], tdev(k))
+
+        quarter = low // 2
+        lows = ((0, quarter), (quarter, low))
+        highs = ((low, low + quarter), (low + quarter, slots))
+        first_up, first_down = [], []
+        for i in (0, 1):
+            loop(far, *lows[i])
+            first_up.append(ring(0, *lows[i], 1))
+            loop(far, *highs[i])
+            first_down.append(ring(0, *highs[i], 3))
         pair[1].wait_recv()
 
         def near_up(c, panel, row):
             rsend[1, c] = mine(1, c, panel, row).astype(BF16)
 
         loop(near_up, low, slots)
-        second_up = send(rsend.at[1, pl.ds(low, low)], rrecv.at[1, pl.ds(low, low)], tdev(1))
+        rest = [ring(1, low, slots, 1)]
         pair[3].wait_recv()
 
         def near_down(c, panel, row):
             rsend[2, c] = mine(3, c, panel, row).astype(BF16)
 
         loop(near_down, 0, low)
-        second_down = send(rsend.at[2, pl.ds(0, low)], rrecv.at[2, pl.ds(0, low)], tdev(3))
-
-        first_up.wait_recv()
+        rest.append(ring(2, 0, low, 3))
 
         def merged_up(c, panel, row):
             rsend[1, c] = (mine(1, c, panel, row) + rrecv[0, c].astype(F32)).astype(BF16)
 
-        loop(merged_up, 0, low)
-        third_up = send(rsend.at[1, pl.ds(0, low)], rrecv.at[1, pl.ds(0, low)], tdev(1))
-        first_down.wait_recv()
-
         def merged_down(c, panel, row):
             rsend[2, c] = (mine(3, c, panel, row) + rrecv[0, c].astype(F32)).astype(BF16)
 
-        loop(merged_down, low, slots)
-        third_down = send(rsend.at[2, pl.ds(low, low)], rrecv.at[2, pl.ds(low, low)], tdev(3))
+        for i in (0, 1):
+            first_up[i].wait_recv()
+            loop(merged_up, *lows[i])
+            rest.append(ring(1, *lows[i], 1))
+            first_down[i].wait_recv()
+            loop(merged_down, *highs[i])
+            rest.append(ring(2, *highs[i], 3))
         pair[0].wait_recv()
         if between is not None:
             between()
-        for copy in (second_up, second_down, third_up, third_down):
+        for copy in rest:
             copy.wait_recv()
         all_tiles = gathered.at[use]
 
@@ -315,22 +332,22 @@
 
         loop(last)
 
-        def half(v, h):
-            return all_tiles.at[seg * 4 + v, pl.ds(h * low, low)]
+        def piece(v, start, stop):
+            return all_tiles.at[seg * 4 + v, pl.ds(start, stop - start)]
 
         def whole(v):
             return all_tiles.at[seg * 4 + v]
 
-        up, down = ring_gather(half, tok, tdev)
         crossing = [send(whole(tok), whole(tok), sibling)]
-        up[1].wait_recv()
+        up, down = ring_gather(piece, (quarter, low, low + quarter, slots), tok, tdev)
+        up[2].wait_recv()
         before = turn(tok, 3)
         crossing.append(send(whole(before), whole(before), sibling))
-        down[1].wait_recv()
+        down[2].wait_recv()
         after = turn(tok, 1)
         crossing.append(send(whole(after), whole(after), sibling))
-        up[2].wait_recv()
-        down[2].wait_recv()
+        for copy in up[3:] + down[3:]:
+            copy.wait_recv()
         far_side = turn(tok, 2)
         crossing.append(send(whole(far_side), whole(far_side), sibling))
         for copy in crossing:
@@ -361,69 +378,57 @@
 
     latents = dense.at[0]
 
-    def decode_block(k, carry):
+    def decode_block(k):
         b = pl.multiple_of(turn(x, k) * BLOCK, BLOCK)
-        decoded[k] = nt(latents[pl.ds(b, BLOCK), :], dec_w[...])
-        return carry
-
-    lax.fori_loop(0, BLOCKS, decode_block, 0)
-
-    def decode(k):
-        return decoded[k]
-
-    far = decode(2)
+        return nt(latents[pl.ds(b, BLOCK), :], dec_w[...])
+
+    far = decode_block(2)
     xs_send[0] = far.astype(BF16)
     first_up = send(xs_send.at[0, pl.ds(0, 64)], xs_recv.at[0, pl.ds(0, 64)], xdev(1))
     first_down = send(xs_send.at[0, pl.ds(64, 64)], xs_recv.at[0, pl.ds(64, 64)], xdev(3))
-    near = decode(1)
-    xs_send[1, 64:, :] = near[64:, :].astype(BF16)
+
+    def decode_near(i, carry):
+        k = turn(i, 3)
+        decoded[k] = decode_block(k)
+        return carry
+
+    lax.fori_loop(0, 3, decode_near, 0)
+    part_up = decoded[1]
+    xs_send[1, 64:, :] = part_up[64:, :].astype(BF16)
     second_up = send(xs_send.at[1, pl.ds(64, 64)], xs_recv.at[1, pl.ds(64, 64)], xdev(1))
-    block_own[0:64, :] = near[:64, :]
-    near = decode(3)
-    xs_send[2, :64, :] = near[:64, :].astype(BF16)
+    block_own[0:64, :] = part_up[:64, :]
+    part_down = decoded[3]
+    xs_send[2, :64, :] = part_down[:64, :].astype(BF16)
     second_down = send(xs_send.at[2, pl.ds(0, 64)], xs_recv.at[2, pl.ds(0, 64)], xdev(3))
-    block_own[64:128, :] = near[64:, :]
+    block_own[64:128, :] = part_down[64:, :]
     first_up.wait_recv()
     xs_send[1, :64, :] = (block_own[0:64, :] + xs_recv[0, :64, :].astype(F32)).astype(BF16)
     third_up = send(xs_send.at[1, pl.ds(0, 64)], xs_recv.at[1, pl.ds(0, 64)], xdev(1))
     first_down.wait_recv()
     xs_send[2, 64:, :] = (block_own[64:128, :] + xs_recv[0, 64:, :].astype(F32)).astype(BF16)
     third_down = send(xs_send.at[2, pl.ds(64, 64)], xs_recv.at[2, pl.ds(64, 64)], xdev(3))
-    block_own[...] = decode(0)
+    block_own[...] = decoded[0]
     for copy in (second_up, second_down, third_up, third_down):
         copy.wait_recv()
     block_own[...] = block_own[...] + xs_recv[1].astype(F32) + xs_recv[2].astype(F32)
 
-    copies = []
-    for k in (1, 2, 3):
-        at = pl.multiple_of(turn(zl, k) * 32, 32)
-        zs_send[k - 1] = block_own[pl.ds(at, 32), :].astype(BF16)
-        copies.append(send(zs_send.at[k - 1], zs_recv.at[k - 1], zdev(k)))
-    quarter = block_own[pl.ds(pl.multiple_of(zl * 32, 32), 32), :]
-    for k in (1, 2, 3):
-        copies[k - 1].wait_recv()
-        quarter = quarter + zs_recv[k - 1].astype(F32)
-    block_own[0:32, :] = quarter
-    copies = []
-    for k in (1, 2, 3):
-        at = pl.multiple_of(turn(y, k) * 8, 8)
-        ys_send[k - 1] = block_own[pl.ds(at, 8), :].astype(BF16)
-        copies.append(send(ys_send.at[k - 1], ys_recv.at[k - 1], ydev(k)))
-    rebuilt = block_own[pl.ds(pl.multiple_of(y * 8, 8), 8), :]
-    for k in (1, 2, 3):
-        copies[k - 1].wait_recv()
-        rebuilt = rebuilt + ys_recv[k - 1].astype(F32)
+    ps_send[...] = block_own[...].astype(BF16).reshape(16, 8, WIDTH)
+    copies = [send(ps_send.at[plane(i, j)], ps_recv.at[spot], pdev(i, j)) for i, j in near]
+    rebuilt = block_own[pl.ds(pl.multiple_of(spot * 8, 8), 8), :]
+    for copy in copies:
+        copy.wait_recv()
+    for i, j in near:
+        rebuilt = rebuilt + ps_recv[plane(i, j)].astype(F32)
 
     error = rebuilt + dec_bias[...] - own_rows[...].astype(F32)
     squared = jnp.sum(jnp.sum(error * error, axis=1, keepdims=True), axis=0, keepdims=True)
-    loss = gather_all(
+    beside, side_sum = gather_all(
         error.astype(BF16), gather_y.at[1], feats.at[1], jnp.broadcast_to(squared, (8, 128))
     )
     errors = feats.at[1]
-    sq_buf[1, me] = loss
+    expand(errors, dec_w)
+    sq_buf[1, me] = side_sum(2, beside)
     loss_copies = group_start(sq_buf.at[1])
-
-    expand(errors, dec_w)
     store_dec = pltpu.make_async_copy(dec_v, dec_out, local_sem.at[7])
     store_enc = pltpu.make_async_copy(enc_v, enc_out, local_sem.at[8])
 
@@ -473,7 +478,7 @@
             low((WIDTH, LOCAL), BF16),
             low((2, 8, 8, 128), F32),
             low((8, WIDTH), BF16),
-            low((2, 4, 8, WIDTH), BF16),
+            low((2, 16, 8, WIDTH), BF16),
             low((2, TOKENS, WIDTH), BF16),
             low((TOKENS, WIDTH), BF16),
             low((PANELS, TOKENS // OWN, OWN, BLOCK), F32),
@@ -488,10 +493,8 @@
             low((BLOCK, WIDTH), F32),
             low((3, BLOCK, WIDTH), BF16),
             low((3, BLOCK, WIDTH), BF16),
-            low((3, 32, WIDTH), BF16),
-            low((3, 32, WIDTH), BF16),
-            low((3, 8, WIDTH), BF16),
-            low((3, 8, WIDTH), BF16),
+            low((16, 8, WIDTH), BF16),
+            low((16, 8, WIDTH), BF16),
             low((3, 4, 8, 128), F32),
             low((WIDTH, LOCAL), BF16),
             low((WIDTH, LOCAL), BF16),

time: 152 us -> 153 us (level)
  Pallas kernels: 141 us -> 144 us
    pallas_call x1, Pallas kernels: 141 us -> 144 us  [step(): pl.pallas_call(functools.partial(kernel, slots), name=f'sae_step_{slots}'...]
where the time goes in v3:
time: 153 us; the launch traced here: 152 us
  Pallas kernels  144 us (94%)
  local copies, waits for them, and re-layouts  4.08 us (3%)
  other arithmetic  2.61 us (2%)
    pallas_call x1, Pallas kernels, step(): pl.pallas_call(functools.partial(kernel, slots), name=f'sae_step_{slots}'...  144 us

profile of v3, /device:TPU:1, one launch (start us, length us, event | category | flops | bytes accessed | tf_op | source)
XLA Modules:
  0.0 152.5 jit_solution(11536740871937011102)
XLA Ops:
  0.6 0.9 compare_reduce_fusion
  1.5 0.1 reshape.200
  1.6 0.1 reshape.199
  1.7 0.1 select_reduce_fusion.1
  1.8 0.1 select_reduce_fusion
  2.0 0.7 add_select_fusion
  2.7 0.1 convert_reduce_fusion
  2.8 0.6 reduce_max.9
  4.1 146.4 %conditional.1 = (bf16[576,1024]{1,0:T(8,128)(2,1)S(1)}, bf16[576,1024]{1,0:T(8,128)(2,1)S(1)}, f32[]{:T(128)}) conditional(s32[]{:T(128)} %clamp.3, (f32[576]{0:T(1024)}, f32[1024]{0:T(1024)}, f32[576]{0:T(1024)}, bf16[1024,576]{0,1:T(8,128)(2,1)}, s32[4,32]{1,0:T(4,128)S(1)}, /*index=5*/bf16[8,576]{1,0:T(8,128)(2,1)}, bf16[8,576]{1,0:T(8,128)(2,1)}, ...), branch_computations={%region_5.6_spmd, %region_6.7_spmd} | conditional | bytes 9248 | solution.py:539
  4.1 0.7 reshape.191.gain_hbm
  4.8 0.7 reshape.193.dec_bias_hbm
  5.5 144.4 %sae_step_20.1 = (f32[8,128]{1,0:T(8,128)S(1)}, bf16[576,1024]{1,0:T(8,128)(2,1)S(1)}, bf16[576,1024]{1,0:T(8,128)(2,1)S(1)}) custom-call(s32[4,32]{1,0:T(4,128)S(1)} %get-tuple-element.39.table, bf16[8,576]{1,0:T(8,128)(2,1)} %get-tuple-element.40.resid_hbm, bf16[8,576]{1,0:T(8,128)(2,1)} %get-tuple-element.41.mlp_hbm, f32[1,576]{1,0:T(1,128)S(1)} %reshape.191.gain_hbm, ...), custom_call_target="tpu_custom_call" | custom-call | tf_op jit(solution)/shard_map/cond/branch_0_fun/sae_step_20/pallas_call | solution.py:461
  150.0 0.5 slice.5
  150.5 1.0 copy.19
  151.5 1.0 copy.20
  (5 shorter events, 0.0 us)

commit v4 on v3

--- a/solution.py
+++ b/solution.py
@@ -20,7 +20,7 @@
 F32 = jnp.float32
 BF16 = jnp.bfloat16
 COPIES = 192
-CAPACITIES = (20, 32)
+CAPACITIES = (16, 20, 32)
 
 
 def gelu_pair(x):
@@ -260,14 +260,17 @@
             lax.fori_loop(start, stop, step, 0)
 
         pair = {}
-        for k in (2, 1, 3, 0):
-            t = turn(tok, k)
+        for ks in ((2,), (1, 3, 0)):
 
             def to_pair(c, panel, row):
-                psend[t, c] = part[panel, row + (1 - seg) * 4 + t].astype(BF16)
+                for k in ks:
+                    t = turn(tok, k)
+                    psend[t, c] = part[panel, row + (1 - seg) * 4 + t].astype(BF16)
 
             loop(to_pair)
-            pair[k] = send(psend.at[t], precv.at[t], sibling)
+            for k in ks:
+                t = turn(tok, k)
+                pair[k] = send(psend.at[t], precv.at[t], sibling)
 
         def mine(k, c, panel, row):
             t = turn(tok, k)

time: 153 us -> 153 us (level)
  no operation moved by 1% of the time
where the time goes in v4:
time: 153 us; the launch traced here: 152 us
  Pallas kernels  144 us (94%)
  local copies, waits for them, and re-layouts  4.08 us (3%)
  other arithmetic  2.61 us (2%)
  between operations  1.98 us (1%)
    pallas_call x1, Pallas kernels, step(): pl.pallas_call(functools.partial(kernel, slots), name=f'sae_step_{slots}'...  144 us

profile of v4, /device:TPU:1, one launch (start us, length us, event | category | flops | bytes accessed | tf_op | source)
XLA Modules:
  0.0 152.3 jit_solution(13622940833311171014)
XLA Ops:
  0.6 0.9 compare_reduce_fusion
  1.5 0.1 reshape.209
  1.6 0.1 reshape.208
  1.7 0.1 select_reduce_fusion.1
  1.8 0.1 select_reduce_fusion
  2.0 0.7 add_select_fusion
  2.7 0.1 convert_reduce_fusion
  2.8 0.6 reduce_max.9
  4.8 145.5 %conditional.1 = (bf16[576,1024]{1,0:T(8,128)(2,1)S(1)}, bf16[576,1024]{1,0:T(8,128)(2,1)S(1)}, f32[]{:T(128)}) conditional(s32[]{:T(128)} %clamp.3, (f32[576]{0:T(1024)}, f32[1024]{0:T(1024)}, f32[576]{0:T(1024)}, bf16[1024,576]{0,1:T(8,128)(2,1)}, s32[4,32]{1,0:T(4,128)S(1)}, /*index=5*/bf16[8,576]{1,0:T(8,128)(2,1)}, ...), branch_computations={%region_5.6_spmd, %region_6.7_spmd, %region_7.8_spmd} | conditional | bytes 9248 | solution.py:542
  4.8 0.7 reshape.200.gain_hbm
  5.5 0.7 reshape.202.dec_bias_hbm
  6.2 143.5 %sae_step_20.1 = (f32[8,128]{1,0:T(8,128)S(1)}, bf16[576,1024]{1,0:T(8,128)(2,1)S(1)}, bf16[576,1024]{1,0:T(8,128)(2,1)S(1)}) custom-call(s32[4,32]{1,0:T(4,128)S(1)} %get-tuple-element.69.table, bf16[8,576]{1,0:T(8,128)(2,1)} %get-tuple-element.70.resid_hbm, bf16[8,576]{1,0:T(8,128)(2,1)} %get-tuple-element.71.mlp_hbm, f32[1,576]{1,0:T(1,128)S(1)} %reshape.200.gain_hbm, ...), custom_call_target="tpu_custom_call" | custom-call | tf_op jit(solution)/shard_map/cond/branch_1_fun/sae_step_20/pallas_call | solution.py:464
  149.7 0.5 slice.8
  150.2 1.0 copy.22
  151.2 1.0 copy.23
  (5 shorter events, 0.0 us)

commit v5 on v4

--- a/solution.py
+++ b/solution.py
@@ -20,7 +20,7 @@
 F32 = jnp.float32
 BF16 = jnp.bfloat16
 COPIES = 192
-CAPACITIES = (16, 20, 32)
+CAPACITIES = (16, 18, 20, 24, 32)
 
 
 def gelu_pair(x):
@@ -144,9 +144,9 @@
             (
                 (mlp_hbm, mlp),
                 (resid_hbm, resid),
-                (gain_hbm, gain),
+                (gain_hbm, gain.at[0]),
                 (enc_bias_hbm, enc_bias),
-                (dec_bias_hbm, dec_bias),
+                (dec_bias_hbm, dec_bias.at[0]),
                 (enc_w_hbm, enc_w),
                 (dec_w_hbm, dec_w),
             )
@@ -512,9 +512,9 @@
         table,
         resid_mid,
         mlp_out,
-        post_gain.reshape(1, WIDTH),
+        post_gain,
         enc_bias.reshape(PANELS, BLOCK),
-        dec_bias.reshape(1, WIDTH),
+        dec_bias,
         enc_weight,
         dec_weight.T,
     )

time: 153 us -> 148 us (0.967); the launches traced: 152 us -> 149 us
  Pallas kernels: 144 us -> 140 us
    pallas_call x1, Pallas kernels: 144 us -> 140 us  [step(): pl.pallas_call(functools.partial(kernel, slots), name=f'sae_step_{slots}'...]
where the time goes in v5:
time: 148 us; the launch traced here: 149 us
  Pallas kernels  140 us (95%)
  between operations  3.28 us (2%)
  local copies, waits for them, and re-layouts  2.7 us (2%)
  other arithmetic  2.61 us (2%)
    pallas_call x1, Pallas kernels, step(): pl.pallas_call(functools.partial(kernel, slots), name=f'sae_step_{slots}'...  140 us

profile of v5, /device:TPU:1, one launch (start us, length us, event | category | flops | bytes accessed | tf_op | source)
XLA Modules:
  0.0 149.0 jit_solution(7123421538878720920)
XLA Ops:
  0.6 0.9 compare_reduce_fusion
  1.5 0.1 reshape.197
  1.6 0.1 reshape.196
  1.7 0.1 select_reduce_fusion.1
  1.8 0.1 select_reduce_fusion
  2.0 0.7 add_select_fusion
  2.7 0.1 convert_reduce_fusion
  2.8 0.6 reduce_max.9
  6.1 140.9 %conditional.1 = (bf16[576,1024]{1,0:T(8,128)(2,1)S(1)}, bf16[576,1024]{1,0:T(8,128)(2,1)S(1)}, f32[]{:T(128)}) conditional(s32[]{:T(128)} %clamp.3, (f32[1024]{0:T(1024)}, bf16[1024,576]{0,1:T(8,128)(2,1)}, s32[4,32]{1,0:T(4,128)S(1)}, bf16[8,576]{1,0:T(8,128)(2,1)}, bf16[8,576]{1,0:T(8,128)(2,1)}, ...), branch_computations={%region_5.6_spmd, %region_6.7_spmd, %region_7.8_spmd, %region_8.9_... | conditional | bytes 32 | solution.py:542
  6.1 140.4 %sae_step_18.1 = (f32[8,128]{1,0:T(8,128)S(1)}, bf16[576,1024]{1,0:T(8,128)(2,1)S(1)}, bf16[576,1024]{1,0:T(8,128)(2,1)S(1)}) custom-call(s32[4,32]{1,0:T(4,128)S(1)} %get-tuple-element.107.table, bf16[8,576]{1,0:T(8,128)(2,1)} %get-tuple-element.108.resid_hbm, bf16[8,576]{1,0:T(8,128)(2,1)} %get-tuple-element.109.mlp_hbm, f32[576]{0:T(1024)} %get-tuple-element.110.gain_hbm, ...), custom_call_target="tpu_custom_call" | custom-call | tf_op jit(solution)/shard_map/cond/branch_1_fun/sae_step_18/pallas_call | solution.py:464
  146.5 0.5 slice.12
  147.0 1.0 copy.28
  148.0 1.0 copy.29
  (5 shorter events, 0.0 us)
